TPU v7x, 32 devices: a whole 2x2x4 slice. The times are simulated.
32 devices in a mesh: ctx: 8 (over y, x, core), ch: 4 (over z).
Axes of the slice: x: 2, y: 2, z: 4, core: 2. Of those that a mesh axis runs over, the one named last changes fastest.
Arguments:
- query_act: bfloat16 [2048, 8192], P('ctx', 'ch'), may hold values from -6 to 6
- key_act: bfloat16 [2048, 8192], P('ctx', 'ch'), may hold values from -6 to 6
- value_act: bfloat16 [2048, 8192], P('ctx', 'ch'), may hold values from -6 to 6
- out_grad: bfloat16 [2048, 8192], P('ctx', 'ch'), may hold values from -6 to 6
- out_weight: bfloat16 [8192, 8192], P('ctx', 'ch'), may hold values from -0.0625 to 0.0625
- token_mask: int32 [2048], P('ctx'), may hold values from 0 to 1, as said below
- decay_rate: float32 [16, 8192], P(None, 'ch'), may hold values from 4.8828125e-05 to 0.033
- residue: float32 [16, 8192], P(None, 'ch'), may hold values from -75 to 75
Outputs:
- query_grad: bfloat16 [2048, 8192], P('ctx', 'ch')
- key_grad: bfloat16 [2048, 8192], P('ctx', 'ch')
- value_grad: bfloat16 [2048, 8192], P('ctx', 'ch')
- filter_grad: float32 [16, 8192], P(None, 'ch')
Inputs may be any that keep to these rules, and one draw needn't show every extreme that they name: `token_mask`: 1 marks a valid token; within each aligned run of 64 positions the valid tokens come first.
All inputs are finite; a program needn't handle non-finite values.
Results may differ from a plain program's by a relative error of at most 0.0015.
Values may be sent and summed in bfloat16 or wider, within the bound.
A program may use at most 192 MiB of HBM per device.

v0:
```python
import jax
import jax.numpy as jnp
from jax import lax
from jax.sharding import PartitionSpec as P


def carried_in(shard, axis, combine, identity, reverse):
    devices, here = (lax.axis_size(axis), lax.axis_index(axis))
    everything = jax.tree.map(lambda part: lax.all_gather(part, axis), shard)
    start = jax.tree.map(
        lambda part, zero: jnp.broadcast_to(jnp.asarray(zero, part.dtype), part.shape),
        shard,
        identity,
    )

    def turn(k, before):
        at = devices - 1 - k if reverse else k
        reached = at > here if reverse else at < here
        new = combine(before, jax.tree.map(lambda part: part[at], everything))
        return jax.tree.map(lambda a, b: jnp.where(reached, a, b), new, before)

    return lax.fori_loop(0, devices, turn, start)


def chain_join(earlier, later):
    return (earlier[0] * later[0], later[0] * earlier[1] + later[1])


def body(query_act, key_act, value_act, out_grad, out_weight, token_mask, decay_rate, residue):
    rows_block = 64
    tokens_here = query_act.shape[0]
    chans = query_act.shape[1]
    modes = decay_rate.shape[0]
    blocks = tokens_here // rows_block
    live = token_mask.astype(jnp.float32)[:, None]
    inputs = live * key_act.astype(jnp.float32) * value_act.astype(jnp.float32)
    root_gain = jnp.sqrt(-jnp.expm1(-2.0 * decay_rate))
    filter_gain = residue * root_gain
    places = jnp.arange(rows_block).astype(jnp.float32)[:, None, None]
    rising = jnp.exp(decay_rate[None] * places)
    falling = jnp.exp(-decay_rate[None] * places)
    step_decay = jnp.exp(-decay_rate)
    trailing = jnp.exp(-decay_rate[None] * (rows_block - places))
    row_ids = lax.broadcasted_iota(jnp.int32, (rows_block, rows_block), 0)
    col_ids = lax.broadcasted_iota(jnp.int32, (rows_block, rows_block), 1)
    lower_ones = (row_ids >= col_ids).astype(jnp.float32)
    upper_ones = (row_ids <= col_ids).astype(jnp.float32)
    zeros = jnp.zeros((modes, chans), jnp.float32)

    def forward_block(carried, block_in):
        scaled = (rising * block_in[:, None, :]).reshape(rows_block, modes * chans)
        summed = jnp.dot(lower_ones, scaled, precision=lax.Precision.HIGHEST).reshape(
            rows_block, modes, chans
        )
        states = falling * summed + falling * step_decay[None] * carried[None]
        return (states[-1], jnp.sum(filter_gain[None] * states, axis=1))

    end_state, conv_local = lax.scan(
        forward_block, zeros, inputs.reshape(blocks, rows_block, chans)
    )
    conv_local = conv_local.reshape(tokens_here, chans)
    full_grad = lax.all_gather(out_grad, "ch", axis=1, tiled=True)
    gate_grad = jnp.dot(
        full_grad,
        lax.all_gather(out_weight, "ctx", axis=0, tiled=True),
        preferred_element_type=jnp.float32,
    )
    conv_grad = gate_grad * query_act.astype(jnp.float32)

    def backward_block(carry, block_in):
        carried, running = carry
        grad_blk, input_blk = block_in
        scaled = (falling * grad_blk[:, None, :]).reshape(rows_block, modes * chans)
        summed = jnp.dot(upper_ones, scaled, precision=lax.Precision.HIGHEST).reshape(
            rows_block, modes, chans
        )
        states = rising * summed + trailing * carried[None]
        running = running + jnp.sum(input_blk[:, None, :] * states, axis=0)
        return ((states[0], running), jnp.sum(filter_gain[None] * states, axis=1))

    (start_state, filter_local), grad_local = lax.scan(
        backward_block,
        (zeros, zeros),
        (conv_grad.reshape(blocks, rows_block, chans), inputs.reshape(blocks, rows_block, chans)),
        reverse=True,
    )
    grad_local = grad_local.reshape(tokens_here, chans)
    span_decay = jnp.exp(-decay_rate * tokens_here)
    forward_in = carried_in(
        (span_decay, end_state), "ctx", chain_join, (jnp.ones_like(span_decay), zeros), False
    )[1]
    backward_in = carried_in(
        (span_decay, start_state), "ctx", chain_join, (jnp.ones_like(span_decay), zeros), True
    )[1]
    token_places = jnp.arange(tokens_here).astype(jnp.float32)[:, None, None]
    conv = conv_local + jnp.sum(
        jnp.exp(-decay_rate[None] * (token_places + 1.0)) * (filter_gain * forward_in)[None], axis=1
    )
    input_grad = grad_local + jnp.sum(
        jnp.exp(-decay_rate[None] * (tokens_here - token_places))
        * (filter_gain * backward_in)[None],
        axis=1,
    )
    query_grad = (gate_grad * conv).astype(jnp.bfloat16)
    key_grad = (live * input_grad * value_act.astype(jnp.float32)).astype(jnp.bfloat16)
    value_grad = (live * input_grad * key_act.astype(jnp.float32)).astype(jnp.bfloat16)
    filter_terms = root_gain * (filter_local + backward_in * step_decay * end_state)
    filter_grad = lax.psum(filter_terms, "ctx")
    return (query_grad, key_grad, value_grad, filter_grad)


def solution(mesh):
    placed = (
        P("ctx", "ch"),
        P("ctx", "ch"),
        P("ctx", "ch"),
        P("ctx", "ch"),
        P("ctx", "ch"),
        P("ctx"),
        P(None, "ch"),
        P(None, "ch"),
    )
    return jax.shard_map(
        body,
        mesh=mesh,
        in_specs=placed,
        out_specs=(P("ctx", "ch"), P("ctx", "ch"), P("ctx", "ch"), P(None, "ch")),
        check_vma=False,
    )
```

profile of v0, /device:TPU:0, one launch (start us, length us, event | category | flops | bytes accessed | tf_op | source)
XLA Modules:
  0.0 719.4 jit_solution(11028100770254350850)
XLA Ops:
  11.2 1.9 convert_multiply_fusion.1
  14.7 100.9 %while.67 = (s32[]{:T(128)}, f32[16,2048]{1,0:T(8,128)S(1)}, f32[4,64,2048]{2,1,0:T(8,128)}, f32[4,64,2048]{2,1,0:T(8,128)S(1)}, f32[16,2048]{1,0:T(8,128)S(1)},...) while((s32[]{:T(128)}, f32[16,2048]{1,0:T(8,128)S(1)}, ...), condition=%wide.region_2.3_spmd.clone.clone, body=%wide.region_0.2_spmd.clone.clone.sunk | while | flops 1629364224 | bytes 79561336 | solution.py:58
  16.1 5.0 copy.28
  21.2 8.5 %fusion.52 = f32[32768,64]{0,1:T(8,128)S(1)} fusion(f32[64,32768]{1,0:T(8,128)S(1)} %bitcast.141), kind=kOutput, calls=%fused_computation.23.clone.1 | convolution fusion | flops 1610620928 | bytes 16777216 | tf_op jit(solution)/shard_map/while/body/eval_jaxpr/dot_general | solution.py:52
  29.7 5.0 copy.29
  34.7 4.3 multiply_reduce_fusion.6
  41.3 5.0 copy.28
  46.3 8.5 %fusion.52 = f32[32768,64]{0,1:T(8,128)S(1)} fusion(f32[64,32768]{1,0:T(8,128)S(1)} %bitcast.141), kind=kOutput, calls=%fused_computation.23.clone.1 | convolution fusion | flops 1610620928 | bytes 16777216 | tf_op jit(solution)/shard_map/while/body/eval_jaxpr/dot_general | solution.py:52
  54.8 5.0 copy.29
  59.9 4.3 multiply_reduce_fusion.6
  66.4 5.0 copy.28
  71.5 8.5 %fusion.52 = f32[32768,64]{0,1:T(8,128)S(1)} fusion(f32[64,32768]{1,0:T(8,128)S(1)} %bitcast.141), kind=kOutput, calls=%fused_computation.23.clone.1 | convolution fusion | flops 1610620928 | bytes 16777216 | tf_op jit(solution)/shard_map/while/body/eval_jaxpr/dot_general | solution.py:52
  80.0 5.0 copy.29
  85.0 4.3 multiply_reduce_fusion.6
  91.6 5.0 copy.28
  96.6 8.5 %fusion.52 = f32[32768,64]{0,1:T(8,128)S(1)} fusion(f32[64,32768]{1,0:T(8,128)S(1)} %bitcast.141), kind=kOutput, calls=%fused_computation.23.clone.1 | convolution fusion | flops 1610620928 | bytes 16777216 | tf_op jit(solution)/shard_map/while/body/eval_jaxpr/dot_general | solution.py:52
  105.1 5.0 copy.29
  110.2 4.3 multiply_reduce_fusion.6
  117.6 136.5 %all-gather.11.cloned.1.call-done = bf16[8192,2048]{1,0:T(8,128)(2,1)} async-done(((bf16[1024,2048]{1,0:T(8,128)(2,1)}), bf16[8192,2048]{1,0:T(8,128)(2,1)}) %all-gather.11.cloned.1.call-update) | async-done | bytes 33554448 | tf_op jit(solution)/shard_map/all_gather | solution.py:65
  254.1 17.9 %convert_multiply_fusion.4 = (f32[256,2048]{1,0:T(8,128)}, f32[256,2048]{1,0:T(8,128)}) fusion(bf16[256,2048]{1,0:T(8,128)(2,1)} %param.16, bf16[256,8192]{1,0:T(8,128)(2,1)} %all-gather.9.cloned.1.call-done, bf16[8192,2048]{1,0:T(8,128)(2,1)} %all-gather.11.cloned.1.call-done), kind=kOutput, calls=%fused_computation.57 | convolution fusion | flops 8590983168 | bytes 42991616 | tf_op jit(solution)/shard_map/dot_general | solution.py:63
  274.3 343.8 %while.68 = (s32[]{:T(128)}, f32[16,2048]{1,0:T(8,128)}, f32[16,2048]{1,0:T(8,128)}, f32[4,64,2048]{2,1,0:T(8,128)}, f32[4,64,2048]{2,1,0:T(8,128)}, /*index=5*/...) while((s32[]{:T(128)}, f32[16,2048]{1,0:T(8,128)}, ...), condition=%wide.region_9.10_spmd.clone.clone.clone, body=%wide.region_6.0_spmd.clone.clone.clone.sunk | while | flops 1639882752 | bytes 212862208 | solution.py:81
  278.7 4.7 copy.30
  283.5 8.8 %fusion.55 = f32[32768,64]{0,1:T(8,128)S(1)} fusion(f32[64,32768]{1,0:T(8,128)S(1)} %bitcast.143), kind=kOutput, calls=%fused_computation.41.clone.1 | convolution fusion | flops 1610620928 | bytes 16777216 | tf_op jit(solution)/shard_map/while/body/eval_jaxpr/dot_general | solution.py:74
  292.3 8.0 %copy.31 = f32[8,8,16,2048]{3,2,1,0:T(8,128)} copy(f32[8,8,16,2048]{3,1,2,0:T(8,128)S(1)} %bitcast.140) | data formatting | bytes 16777216 | tf_op jit(solution)/shard_map/while
  300.3 10.9 %multiply_reduce_fusion.7 = (f32[64,2048]{1,0:T(8,128)S(1)}, f32[64,16,2048]{2,1,0:T(8,128)}, f32[64,16,2048]{2,1,0:T(8,128)S(1)}, f32[64,16,2048]{2,1,0:T(8,128)}) fusion(f32[16,2048]{1,0:T(8,128)} %copy-done.7, f32[16,2048]{1,0:T(8,128)} %get-tuple-element.1005, f32[64]{0:T(128)S(1)} %get-tuple-element.1028, f32[16,2048]{1,0:T(8,128)} %copy-done, ...), kind=kLoop, calls=%fused_computation.35.clone.1 | loop fusion | flops 14548992 | bytes 34603520 | tf_op jit(solution)/shard_map/while/body/eval_jaxpr/reduce_sum | solution.py:79
  312.8 4.3 mul.700
  317.1 11.7 %copy.32 = f32[8,8,16,2048]{3,1,2,0:T(8,128)} copy(f32[8,8,16,2048]{3,2,1,0:T(8,128)} %bitcast.148) | data formatting | bytes 16777216 | tf_op jit(solution)/shard_map/while
  328.7 11.7 %copy.33 = f32[8,8,16,2048]{3,1,2,0:T(8,128)} copy(f32[8,8,16,2048]{3,2,1,0:T(8,128)} %bitcast.145) | data formatting | bytes 16777216 | tf_op jit(solution)/shard_map/while
  340.4 8.2 %copy.34 = f32[8,8,16,2048]{3,1,2,0:T(8,128)} copy(f32[8,8,16,2048]{3,2,1,0:T(8,128)S(1)} %bitcast.144) | data formatting | bytes 16777216 | tf_op jit(solution)/shard_map/while
  348.6 9.5 %fusion.56 = f32[32768]{0:T(1024)S(1)} fusion(f32[64,32768]{1,0:T(8,128)} %bitcast.149, f32[64,32768]{1,0:T(8,128)} %bitcast.150, f32[32768,64]{0,1:T(8,128)S(1)} %fusion.55, f32[64,32768]{1,0:T(8,128)} %bitcast.151, f32[32768]{0:T(1024)S(1)} %bitcast.153), kind=kLoop, calls=%fused_computation.31.clone.1 | loop fusion | flops 10452992 | bytes 33816576 | tf_op jit(solution)/shard_map/while/body/eval_jaxpr/reduce_sum | solution.py:78
  363.6 4.7 copy.30
  368.4 9.0 %fusion.55 = f32[32768,64]{0,1:T(8,128)S(1)} fusion(f32[64,32768]{1,0:T(8,128)S(1)} %bitcast.143), kind=kOutput, calls=%fused_computation.41.clone.1 | convolution fusion | flops 1610620928 | bytes 16777216 | tf_op jit(solution)/shard_map/while/body/eval_jaxpr/dot_general | solution.py:74
  377.4 8.0 %copy.31 = f32[8,8,16,2048]{3,2,1,0:T(8,128)} copy(f32[8,8,16,2048]{3,1,2,0:T(8,128)S(1)} %bitcast.140) | data formatting | bytes 16777216 | tf_op jit(solution)/shard_map/while
  385.4 10.7 %multiply_reduce_fusion.7 = (f32[64,2048]{1,0:T(8,128)S(1)}, f32[64,16,2048]{2,1,0:T(8,128)}, f32[64,16,2048]{2,1,0:T(8,128)S(1)}, f32[64,16,2048]{2,1,0:T(8,128)}) fusion(f32[16,2048]{1,0:T(8,128)} %copy-done.7, f32[16,2048]{1,0:T(8,128)} %get-tuple-element.1005, f32[64]{0:T(128)S(1)} %get-tuple-element.1028, f32[16,2048]{1,0:T(8,128)} %copy-done, ...), kind=kLoop, calls=%fused_computation.35.clone.1 | loop fusion | flops 14548992 | bytes 34603520 | tf_op jit(solution)/shard_map/while/body/eval_jaxpr/reduce_sum | solution.py:79
  397.6 4.3 mul.700
  402.0 11.7 %copy.32 = f32[8,8,16,2048]{3,1,2,0:T(8,128)} copy(f32[8,8,16,2048]{3,2,1,0:T(8,128)} %bitcast.148) | data formatting | bytes 16777216 | tf_op jit(solution)/shard_map/while
  413.6 11.7 %copy.33 = f32[8,8,16,2048]{3,1,2,0:T(8,128)} copy(f32[8,8,16,2048]{3,2,1,0:T(8,128)} %bitcast.145) | data formatting | bytes 16777216 | tf_op jit(solution)/shard_map/while
  425.3 8.2 %copy.34 = f32[8,8,16,2048]{3,1,2,0:T(8,128)} copy(f32[8,8,16,2048]{3,2,1,0:T(8,128)S(1)} %bitcast.144) | data formatting | bytes 16777216 | tf_op jit(solution)/shard_map/while
  433.6 9.5 %fusion.56 = f32[32768]{0:T(1024)S(1)} fusion(f32[64,32768]{1,0:T(8,128)} %bitcast.149, f32[64,32768]{1,0:T(8,128)} %bitcast.150, f32[32768,64]{0,1:T(8,128)S(1)} %fusion.55, f32[64,32768]{1,0:T(8,128)} %bitcast.151, f32[32768]{0:T(1024)S(1)} %bitcast.153), kind=kLoop, calls=%fused_computation.31.clone.1 | loop fusion | flops 10452992 | bytes 33816576 | tf_op jit(solution)/shard_map/while/body/eval_jaxpr/reduce_sum | solution.py:78
  448.7 4.7 copy.30
  453.5 8.8 %fusion.55 = f32[32768,64]{0,1:T(8,128)S(1)} fusion(f32[64,32768]{1,0:T(8,128)S(1)} %bitcast.143), kind=kOutput, calls=%fused_computation.41.clone.1 | convolution fusion | flops 1610620928 | bytes 16777216 | tf_op jit(solution)/shard_map/while/body/eval_jaxpr/dot_general | solution.py:74
  462.2 8.0 %copy.31 = f32[8,8,16,2048]{3,2,1,0:T(8,128)} copy(f32[8,8,16,2048]{3,1,2,0:T(8,128)S(1)} %bitcast.140) | data formatting | bytes 16777216 | tf_op jit(solution)/shard_map/while
  470.2 10.7 %multiply_reduce_fusion.7 = (f32[64,2048]{1,0:T(8,128)S(1)}, f32[64,16,2048]{2,1,0:T(8,128)}, f32[64,16,2048]{2,1,0:T(8,128)S(1)}, f32[64,16,2048]{2,1,0:T(8,128)}) fusion(f32[16,2048]{1,0:T(8,128)} %copy-done.7, f32[16,2048]{1,0:T(8,128)} %get-tuple-element.1005, f32[64]{0:T(128)S(1)} %get-tuple-element.1028, f32[16,2048]{1,0:T(8,128)} %copy-done, ...), kind=kLoop, calls=%fused_computation.35.clone.1 | loop fusion | flops 14548992 | bytes 34603520 | tf_op jit(solution)/shard_map/while/body/eval_jaxpr/reduce_sum | solution.py:79
  482.5 4.3 mul.700
  486.8 11.7 %copy.32 = f32[8,8,16,2048]{3,1,2,0:T(8,128)} copy(f32[8,8,16,2048]{3,2,1,0:T(8,128)} %bitcast.148) | data formatting | bytes 16777216 | tf_op jit(solution)/shard_map/while
  498.5 11.7 %copy.33 = f32[8,8,16,2048]{3,1,2,0:T(8,128)} copy(f32[8,8,16,2048]{3,2,1,0:T(8,128)} %bitcast.145) | data formatting | bytes 16777216 | tf_op jit(solution)/shard_map/while
  510.2 8.4 %copy.34 = f32[8,8,16,2048]{3,1,2,0:T(8,128)} copy(f32[8,8,16,2048]{3,2,1,0:T(8,128)S(1)} %bitcast.144) | data formatting | bytes 16777216 | tf_op jit(solution)/shard_map/while
  518.6 9.5 %fusion.56 = f32[32768]{0:T(1024)S(1)} fusion(f32[64,32768]{1,0:T(8,128)} %bitcast.149, f32[64,32768]{1,0:T(8,128)} %bitcast.150, f32[32768,64]{0,1:T(8,128)S(1)} %fusion.55, f32[64,32768]{1,0:T(8,128)} %bitcast.151, f32[32768]{0:T(1024)S(1)} %bitcast.153), kind=kLoop, calls=%fused_computation.31.clone.1 | loop fusion | flops 10452992 | bytes 33816576 | tf_op jit(solution)/shard_map/while/body/eval_jaxpr/reduce_sum | solution.py:78
  533.5 4.7 copy.30
  538.3 8.8 %fusion.55 = f32[32768,64]{0,1:T(8,128)S(1)} fusion(f32[64,32768]{1,0:T(8,128)S(1)} %bitcast.143), kind=kOutput, calls=%fused_computation.41.clone.1 | convolution fusion | flops 1610620928 | bytes 16777216 | tf_op jit(solution)/shard_map/while/body/eval_jaxpr/dot_general | solution.py:74
  547.1 8.0 %copy.31 = f32[8,8,16,2048]{3,2,1,0:T(8,128)} copy(f32[8,8,16,2048]{3,1,2,0:T(8,128)S(1)} %bitcast.140) | data formatting | bytes 16777216 | tf_op jit(solution)/shard_map/while
  555.1 10.9 %multiply_reduce_fusion.7 = (f32[64,2048]{1,0:T(8,128)S(1)}, f32[64,16,2048]{2,1,0:T(8,128)}, f32[64,16,2048]{2,1,0:T(8,128)S(1)}, f32[64,16,2048]{2,1,0:T(8,128)}) fusion(f32[16,2048]{1,0:T(8,128)} %copy-done.7, f32[16,2048]{1,0:T(8,128)} %get-tuple-element.1005, f32[64]{0:T(128)S(1)} %get-tuple-element.1028, f32[16,2048]{1,0:T(8,128)} %copy-done, ...), kind=kLoop, calls=%fused_computation.35.clone.1 | loop fusion | flops 14548992 | bytes 34603520 | tf_op jit(solution)/shard_map/while/body/eval_jaxpr/reduce_sum | solution.py:79
  567.5 4.3 mul.700
  571.9 11.7 %copy.32 = f32[8,8,16,2048]{3,1,2,0:T(8,128)} copy(f32[8,8,16,2048]{3,2,1,0:T(8,128)} %bitcast.148) | data formatting | bytes 16777216 | tf_op jit(solution)/shard_map/while
  583.5 11.7 %copy.33 = f32[8,8,16,2048]{3,1,2,0:T(8,128)} copy(f32[8,8,16,2048]{3,2,1,0:T(8,128)} %bitcast.145) | data formatting | bytes 16777216 | tf_op jit(solution)/shard_map/while
  595.2 8.2 %copy.34 = f32[8,8,16,2048]{3,1,2,0:T(8,128)} copy(f32[8,8,16,2048]{3,2,1,0:T(8,128)S(1)} %bitcast.144) | data formatting | bytes 16777216 | tf_op jit(solution)/shard_map/while
  603.4 9.5 %fusion.56 = f32[32768]{0:T(1024)S(1)} fusion(f32[64,32768]{1,0:T(8,128)} %bitcast.149, f32[64,32768]{1,0:T(8,128)} %bitcast.150, f32[32768,64]{0,1:T(8,128)S(1)} %fusion.55, f32[64,32768]{1,0:T(8,128)} %bitcast.151, f32[32768]{0:T(1024)S(1)} %bitcast.153), kind=kLoop, calls=%fused_computation.31.clone.1 | loop fusion | flops 10452992 | bytes 33816576 | tf_op jit(solution)/shard_map/while/body/eval_jaxpr/reduce_sum | solution.py:78
  618.2 13.6 %while.65 = (s32[]{:T(128)}, f32[16,2048]{1,0:T(8,128)}, s32[]{:T(128)}, f32[8,16,2048]{2,1,0:T(8,128)}, f32[8,16,2048]{2,1,0:T(8,128)}, /*index=5*/s32[]{:T(128)}, s32[]{:T(128)}) while((s32[]{:T(128)}, f32[16,2048]{1,0:T(8,128)}, s32[]{:T(128)}, f32[8,16,2048]{2,1,0:T(8,128)}, f32[8,16,2048]{2,1,0:T(8,128)}, ...), condition=%wide.region_4.5_spmd.clone, body=%wide.region_3.4_spmd.clone.sunk | while | flops 131076 | bytes 524397 | solution.py:22
  631.8 9.8 %all-gather.17.cloned.1.call-done = f32[128,2048]{1,0:T(8,128)} async-done(((f32[16,2048]{1,0:T(8,128)}), f32[128,2048]{1,0:T(8,128)}) %all-gather.17.cloned.1.call-update) | async-done | bytes 1048592 | tf_op jit(solution)/shard_map/all_gather | solution.py:9
  641.6 13.5 %while.66 = (s32[]{:T(128)}, f32[16,2048]{1,0:T(8,128)}, s32[]{:T(128)}, f32[8,16,2048]{2,1,0:T(8,128)}, f32[8,16,2048]{2,1,0:T(8,128)}, /*index=5*/s32[]{:T(128)}, s32[]{:T(128)}, s32[]{:T(128)}, s32[]{:T(128)}) while((s32[]{:T(128)}, f32[16,2048]{1,0:T(8,128)}, s32[]{:T(128)}, f32[8,16,2048]{2,1,0:T(8,128)}, ...), condition=%wide.region_11.12_spmd.clone, body=%wide.region_10.11_spmd.clone.sunk | while | flops 131080 | bytes 524459 | solution.py:22
  655.1 1.9 add_multiply_fusion
  657.1 21.9 %multiply_reduce_fusion.2 = (f32[256,2048]{1,0:T(8,128)S(1)}, f32[256,2048]{1,0:T(8,128)S(1)}) fusion(f32[16,2048]{1,0:T(8,128)S(1)} %get-tuple-element.781, f32[256]{0:T(256)S(1)} %copy-done.20, f32[16,2048]{1,0:T(8,128)S(1)} %get-tuple-element.1121, f32[16,2048]{1,0:T(8,128)S(1)} %get-tuple-element.782, f32[256]{0:T(256)} %convert_add_fusion), kind=kLoop, calls=%fused_computation.44 | loop fusion | flops 49283072 | bytes 4589568 | tf_op jit(solution)/shard_map/reduce_sum | solution.py:99
  679.1 3.0 fusion.27
  682.1 28.6 %all-reduce.2.cloned.1.call-done = f32[16,2048]{1,0:T(8,128)} async-done(((f32[16,2048]{1,0:T(8,128)}), f32[16,2048]{1,0:T(8,128)}) %all-reduce.2.cloned.1.call-update) | async-done | bytes 131088 | tf_op jit(solution)/shard_map/psum | solution.py:108
  (197 shorter events, 74.4 us)
Async XLA Ops:
  7.2 7.6 %copy-start.4 = (f32[16,2048]{1,0:T(8,128)S(1)}, f32[16,2048]{1,0:T(8,128)}, u32[]{:S(2)}) copy-start(f32[16,2048]{1,0:T(8,128)} %param.22) | copy-start | bytes 393220
  7.2 110.4 %all-gather.9.cloned.1.call-start = ((), (), s32[]{:S(2)}) async-start(), calls=%async_computation | async-start | bytes 5242880 | tf_op jit(solution)/shard_map/all_gather | solution.py:62
  7.9 246.2 %all-gather.11.cloned.1.call-start = ((), (), s32[]{:S(2)}) async-start(), calls=%async_computation.1 | async-start | bytes 37748736 | tf_op jit(solution)/shard_map/all_gather | solution.py:65
  8.7 609.5 %all-gather.13.cloned.1.call-start = ((), (), s32[]{:S(2)}) async-start(), calls=%async_computation.3 | async-start | bytes 1179648 | tf_op jit(solution)/shard_map/all_gather | solution.py:9
  10.5 607.8 %all-gather.15.cloned.1.call-start = ((), (), s32[]{:S(2)}) async-start(), calls=%async_computation.4 | async-start | bytes 1179648 | tf_op jit(solution)/shard_map/all_gather | solution.py:9
  11.2 1.9 copy-start.18
  115.7 0.7 copy-start.10
  116.3 525.3 %all-gather.17.cloned.1.call-start = ((), (), s32[]{:S(2)}) async-start(), calls=%async_computation.5 | async-start | bytes 1179648 | tf_op jit(solution)/shard_map/all_gather | solution.py:9
  274.3 382.7 %copy-start.20 = (f32[256]{0:T(256)S(1)}, f32[256]{0:T(256)}, u32[]{:S(2)}) copy-start(f32[256]{0:T(256)} %convert_subtract_fusion) | copy-start | bytes 3076
  274.5 4.2 copy-start
  274.5 4.2 copy-start.2
  274.5 4.2 copy-start.5
  274.5 4.2 copy-start.7
  340.4 8.2 %copy-start.9 = (f32[2,16,8,128]{3,1,2,0:T(8,128)S(1)}, f32[2,16,8,128]{3,1,2,0:T(8,128)}, u32[]{:S(2)}) copy-start(f32[2,16,8,128]{3,1,2,0:T(8,128)} %copy.35) | copy-start | bytes 393220 | tf_op jit(solution)/shard_map/while
  348.6 9.5 %copy-start.13 = (f32[16,2048]{1,0:T(8,128)S(1)}, f32[16,2048]{1,0:T(8,128)}, u32[]{:S(2)}) copy-start(f32[16,2048]{1,0:T(8,128)} %get-tuple-element.1006) | copy-start | bytes 393220 | tf_op jit(solution)/shard_map/while
  348.6 10.5 %copy-start.1 = (f32[16,2048]{1,0:T(8,128)S(1)}, f32[16,2048]{1,0:T(8,128)}, u32[]{:S(2)}) copy-start(f32[16,2048]{1,0:T(8,128)} %copy-done) | copy-start | bytes 393220 | tf_op jit(solution)/shard_map/while
  348.6 10.5 %copy-start.3 = (f32[4,64,2048]{2,1,0:T(8,128)S(1)}, f32[4,64,2048]{2,1,0:T(8,128)}, u32[]{:S(2)}) copy-start(f32[4,64,2048]{2,1,0:T(8,128)} %copy-done.2) | copy-start | bytes 6291460 | tf_op jit(solution)/shard_map/while
  348.6 10.5 %copy-start.6 = (f32[16,2048]{1,0:T(8,128)S(1)}, f32[16,2048]{1,0:T(8,128)}, u32[]{:S(2)}) copy-start(f32[16,2048]{1,0:T(8,128)} %copy-done.5) | copy-start | bytes 393220 | tf_op jit(solution)/shard_map/while
  348.6 10.5 %copy-start.8 = (f32[16,2048]{1,0:T(8,128)S(1)}, f32[16,2048]{1,0:T(8,128)}, u32[]{:S(2)}) copy-start(f32[16,2048]{1,0:T(8,128)} %copy-done.7) | copy-start | bytes 393220 | tf_op jit(solution)/shard_map/while
  358.2 0.9 copy-start.14
  359.4 4.2 copy-start
  359.4 4.2 copy-start.2
  359.4 4.2 copy-start.5
  359.4 4.2 copy-start.7
  425.3 8.2 %copy-start.9 = (f32[2,16,8,128]{3,1,2,0:T(8,128)S(1)}, f32[2,16,8,128]{3,1,2,0:T(8,128)}, u32[]{:S(2)}) copy-start(f32[2,16,8,128]{3,1,2,0:T(8,128)} %copy.35) | copy-start | bytes 393220 | tf_op jit(solution)/shard_map/while
  433.5 9.5 %copy-start.13 = (f32[16,2048]{1,0:T(8,128)S(1)}, f32[16,2048]{1,0:T(8,128)}, u32[]{:S(2)}) copy-start(f32[16,2048]{1,0:T(8,128)} %get-tuple-element.1006) | copy-start | bytes 393220 | tf_op jit(solution)/shard_map/while
  433.5 10.5 %copy-start.1 = (f32[16,2048]{1,0:T(8,128)S(1)}, f32[16,2048]{1,0:T(8,128)}, u32[]{:S(2)}) copy-start(f32[16,2048]{1,0:T(8,128)} %copy-done) | copy-start | bytes 393220 | tf_op jit(solution)/shard_map/while
  433.5 10.5 %copy-start.3 = (f32[4,64,2048]{2,1,0:T(8,128)S(1)}, f32[4,64,2048]{2,1,0:T(8,128)}, u32[]{:S(2)}) copy-start(f32[4,64,2048]{2,1,0:T(8,128)} %copy-done.2) | copy-start | bytes 6291460 | tf_op jit(solution)/shard_map/while
  433.5 10.5 %copy-start.6 = (f32[16,2048]{1,0:T(8,128)S(1)}, f32[16,2048]{1,0:T(8,128)}, u32[]{:S(2)}) copy-start(f32[16,2048]{1,0:T(8,128)} %copy-done.5) | copy-start | bytes 393220 | tf_op jit(solution)/shard_map/while
  433.5 10.5 %copy-start.8 = (f32[16,2048]{1,0:T(8,128)S(1)}, f32[16,2048]{1,0:T(8,128)}, u32[]{:S(2)}) copy-start(f32[16,2048]{1,0:T(8,128)} %copy-done.7) | copy-start | bytes 393220 | tf_op jit(solution)/shard_map/while
  443.1 0.9 copy-start.14
  444.4 4.2 copy-start
  444.4 4.2 copy-start.2
  444.4 4.2 copy-start.5
  444.5 4.2 copy-start.7
  510.2 8.4 %copy-start.9 = (f32[2,16,8,128]{3,1,2,0:T(8,128)S(1)}, f32[2,16,8,128]{3,1,2,0:T(8,128)}, u32[]{:S(2)}) copy-start(f32[2,16,8,128]{3,1,2,0:T(8,128)} %copy.35) | copy-start | bytes 393220 | tf_op jit(solution)/shard_map/while
  518.6 9.5 %copy-start.13 = (f32[16,2048]{1,0:T(8,128)S(1)}, f32[16,2048]{1,0:T(8,128)}, u32[]{:S(2)}) copy-start(f32[16,2048]{1,0:T(8,128)} %get-tuple-element.1006) | copy-start | bytes 393220 | tf_op jit(solution)/shard_map/while
  518.6 10.4 %copy-start.1 = (f32[16,2048]{1,0:T(8,128)S(1)}, f32[16,2048]{1,0:T(8,128)}, u32[]{:S(2)}) copy-start(f32[16,2048]{1,0:T(8,128)} %copy-done) | copy-start | bytes 393220 | tf_op jit(solution)/shard_map/while
  518.6 10.4 %copy-start.3 = (f32[4,64,2048]{2,1,0:T(8,128)S(1)}, f32[4,64,2048]{2,1,0:T(8,128)}, u32[]{:S(2)}) copy-start(f32[4,64,2048]{2,1,0:T(8,128)} %copy-done.2) | copy-start | bytes 6291460 | tf_op jit(solution)/shard_map/while
  518.6 10.4 %copy-start.6 = (f32[16,2048]{1,0:T(8,128)S(1)}, f32[16,2048]{1,0:T(8,128)}, u32[]{:S(2)}) copy-start(f32[16,2048]{1,0:T(8,128)} %copy-done.5) | copy-start | bytes 393220 | tf_op jit(solution)/shard_map/while
  518.6 10.4 %copy-start.8 = (f32[16,2048]{1,0:T(8,128)S(1)}, f32[16,2048]{1,0:T(8,128)}, u32[]{:S(2)}) copy-start(f32[16,2048]{1,0:T(8,128)} %copy-done.7) | copy-start | bytes 393220 | tf_op jit(solution)/shard_map/while
  528.2 0.8 copy-start.14
  529.2 4.2 copy-start
  529.2 4.2 copy-start.2
  529.3 4.2 copy-start.5
  529.3 4.2 copy-start.7
  595.2 8.2 %copy-start.9 = (f32[2,16,8,128]{3,1,2,0:T(8,128)S(1)}, f32[2,16,8,128]{3,1,2,0:T(8,128)}, u32[]{:S(2)}) copy-start(f32[2,16,8,128]{3,1,2,0:T(8,128)} %copy.35) | copy-start | bytes 393220 | tf_op jit(solution)/shard_map/while
  603.4 9.5 %copy-start.13 = (f32[16,2048]{1,0:T(8,128)S(1)}, f32[16,2048]{1,0:T(8,128)}, u32[]{:S(2)}) copy-start(f32[16,2048]{1,0:T(8,128)} %get-tuple-element.1006) | copy-start | bytes 393220 | tf_op jit(solution)/shard_map/while
  603.4 10.5 %copy-start.1 = (f32[16,2048]{1,0:T(8,128)S(1)}, f32[16,2048]{1,0:T(8,128)}, u32[]{:S(2)}) copy-start(f32[16,2048]{1,0:T(8,128)} %copy-done) | copy-start | bytes 393220 | tf_op jit(solution)/shard_map/while
  603.4 10.5 %copy-start.3 = (f32[4,64,2048]{2,1,0:T(8,128)S(1)}, f32[4,64,2048]{2,1,0:T(8,128)}, u32[]{:S(2)}) copy-start(f32[4,64,2048]{2,1,0:T(8,128)} %copy-done.2) | copy-start | bytes 6291460 | tf_op jit(solution)/shard_map/while
  603.4 10.5 %copy-start.6 = (f32[16,2048]{1,0:T(8,128)S(1)}, f32[16,2048]{1,0:T(8,128)}, u32[]{:S(2)}) copy-start(f32[16,2048]{1,0:T(8,128)} %copy-done.5) | copy-start | bytes 393220 | tf_op jit(solution)/shard_map/while
  603.4 10.5 %copy-start.8 = (f32[16,2048]{1,0:T(8,128)S(1)}, f32[16,2048]{1,0:T(8,128)}, u32[]{:S(2)}) copy-start(f32[16,2048]{1,0:T(8,128)} %copy-done.7) | copy-start | bytes 393220 | tf_op jit(solution)/shard_map/while
  613.0 0.9 copy-start.14
  618.1 92.5 %all-reduce.2.cloned.1.call-start = ((), (), s32[]{:S(2)}) async-start(), calls=%async_computation.2 | async-start | bytes 262144 | tf_op jit(solution)/shard_map/psum | solution.py:108
  657.0 22.0 %copy-start.11 = (f32[4,64,2048]{2,1,0:T(8,128)S(1)}, f32[4,64,2048]{2,1,0:T(8,128)}, u32[]{:S(2)}) copy-start(f32[4,64,2048]{2,1,0:T(8,128)} %get-tuple-element.500) | copy-start | bytes 6291460
  657.0 22.0 %copy-start.12 = (f32[4,64,2048]{2,1,0:T(8,128)S(1)}, f32[4,64,2048]{2,1,0:T(8,128)}, u32[]{:S(2)}) copy-start(f32[4,64,2048]{2,1,0:T(8,128)} %get-tuple-element.497) | copy-start | bytes 6291460
  657.1 22.0 %copy-start.15 = (bf16[256,2048]{1,0:T(8,128)(2,1)S(1)}, bf16[256,2048]{1,0:T(8,128)(2,1)}, u32[]{:S(2)}) copy-start(bf16[256,2048]{1,0:T(8,128)(2,1)} %param.17) | copy-start | bytes 3145732
  657.1 22.0 %copy-start.16 = (bf16[256,2048]{1,0:T(8,128)(2,1)S(1)}, bf16[256,2048]{1,0:T(8,128)(2,1)}, u32[]{:S(2)}) copy-start(bf16[256,2048]{1,0:T(8,128)(2,1)} %param.18) | copy-start | bytes 3145732
  657.1 22.0 %copy-start.17 = (f32[256,2048]{1,0:T(8,128)S(1)}, f32[256,2048]{1,0:T(8,128)}, u32[]{:S(2)}) copy-start(f32[256,2048]{1,0:T(8,128)} %get-tuple-element.788) | copy-start | bytes 6291460
  657.1 22.0 %copy-start.19 = (f32[256]{0:T(256)S(1)}, f32[256]{0:T(256)}, u32[]{:S(2)}) copy-start(f32[256]{0:T(256)} %copy-done.18) | copy-start | bytes 3076
Sparse Core Ops, SparseCore 0:
  9.6 83.4 all-gather.8
  94.9 159.1 all-gather.10
  256.6 23.3 all-gather.12
  282.3 23.3 all-gather.14
  618.2 23.3 all-gather.16
  657.1 53.4 all-reduce.1
where the time goes:
time: 721 us; the launch traced here: 719 us
  local copies, waits for them, and re-layouts  266 us (37%)
  waiting for transfers between devices  176 us (24%)
  other arithmetic  169 us (23%)
  matrix products  87.4 us (12%)
  between operations  14.7 us (2%)
    while x120, local copies, waits for them, and re-layouts  225 us
    all_gather x1, waiting for transfers between devices, body(): lax.all_gather(out_weight, 'ctx', axis=0, tiled=True)  137 us
    reduce_sum x4, other arithmetic, backward_block(): return ((states[0], running), jnp.sum(filter_gain[None] * states, axis=1))  43.2 us
    reduce_sum x4, other arithmetic, backward_block(): running = running + jnp.sum(input_blk[:, None, :] * states, axis=0)  37.9 us
    dot_general x4, matrix products, backward_block(): jnp.dot(upper_ones, scaled, precision=lax.Precision.HIGHEST)  35.5 us
    dot_general x4, matrix products, forward_block(): jnp.dot(lower_ones, scaled, precision=lax.Precision.HIGHEST)  34 us
    psum x1, waiting for transfers between devices, body(): filter_grad = lax.psum(filter_terms, 'ctx')  28.6 us
    select_n x16, other arithmetic, turn(): return jax.tree.map(lambda a, b: jnp.where(reached, a, b), new, before)  27.1 us
  transfers between devices with their start and end apart: 6, of which 3 were waited for; matrix products, arithmetic and copies ran while one was open for 70% of the time, Pallas kernels for 0%

commit v1 on v0

--- a/solution.py
+++ b/solution.py
@@ -105,7 +105,7 @@
     key_grad = (live * input_grad * value_act.astype(jnp.float32)).astype(jnp.bfloat16)
     value_grad = (live * input_grad * key_act.astype(jnp.float32)).astype(jnp.bfloat16)
     filter_terms = root_gain * (filter_local + backward_in * step_decay * end_state)
-    filter_grad = lax.psum(filter_terms, "ctx")
+    filter_grad = jnp.sum(lax.all_gather(filter_terms, "ctx"), axis=0)
     return (query_grad, key_grad, value_grad, filter_grad)
 
 

time: 721 us -> 693 us (0.961)
  waiting for transfers between devices: 176 us -> 148 us
    psum x1 -> x0, waiting for transfers between devices: 28.6 us -> none  [body(): filter_grad = lax.psum(filter_terms, 'ctx')]
  transfers between devices with their start and end apart: 6 -> 6, of which waited for: 3 -> 2; matrix products, arithmetic and copies ran while one was open for 70% -> 73% of each run, Pallas kernels for 0% -> 0%
where the time goes in v1:
time: 693 us; the launch traced here: 691 us
  local copies, waits for them, and re-layouts  264 us (38%)
  other arithmetic  170 us (25%)
  waiting for transfers between devices  148 us (21%)
  matrix products  87.4 us (13%)
  between operations  14.7 us (2%)
    while x120, local copies, waits for them, and re-layouts  225 us
    all_gather x1, waiting for transfers between devices, body(): lax.all_gather(out_weight, 'ctx', axis=0, tiled=True)  137 us
    reduce_sum x4, other arithmetic, backward_block(): return ((states[0], running), jnp.sum(filter_gain[None] * states, axis=1))  43.2 us
    reduce_sum x4, other arithmetic, backward_block(): running = running + jnp.sum(input_blk[:, None, :] * states, axis=0)  37.9 us
    dot_general x4, matrix products, backward_block(): jnp.dot(upper_ones, scaled, precision=lax.Precision.HIGHEST)  35.5 us
    dot_general x4, matrix products, forward_block(): jnp.dot(lower_ones, scaled, precision=lax.Precision.HIGHEST)  34 us
    select_n x16, other arithmetic, turn(): return jax.tree.map(lambda a, b: jnp.where(reached, a, b), new, before)  27.1 us
    reduce_sum x1, other arithmetic, body(): jnp.sum(jnp.exp(-decay_rate[None] * (tokens_here - token_places)) * (filt...  21.9 us
  transfers between devices with their start and end apart: 6, of which 2 were waited for; matrix products, arithmetic and copies ran while one was open for 73% of the time, Pallas kernels for 0%

profile of v1, /device:TPU:0, one launch (start us, length us, event | category | flops | bytes accessed | tf_op | source)
XLA Modules:
  0.0 691.3 jit_solution(15695479811932601320)
XLA Ops:
  11.2 1.9 convert_multiply_fusion.1
  14.7 100.9 %while.67 = (s32[]{:T(128)}, f32[16,2048]{1,0:T(8,128)S(1)}, f32[4,64,2048]{2,1,0:T(8,128)}, f32[4,64,2048]{2,1,0:T(8,128)S(1)}, f32[16,2048]{1,0:T(8,128)S(1)},...) while((s32[]{:T(128)}, f32[16,2048]{1,0:T(8,128)S(1)}, ...), condition=%wide.region_2.3_spmd.clone.clone, body=%wide.region_0.2_spmd.clone.clone.sunk | while | flops 1629364224 | bytes 79561336 | solution.py:58
  16.1 5.0 copy.28
  21.2 8.5 %fusion.52 = f32[32768,64]{0,1:T(8,128)S(1)} fusion(f32[64,32768]{1,0:T(8,128)S(1)} %bitcast.142), kind=kOutput, calls=%fused_computation.23.clone.1 | convolution fusion | flops 1610620928 | bytes 16777216 | tf_op jit(solution)/shard_map/while/body/eval_jaxpr/dot_general | solution.py:52
  29.7 5.0 copy.29
  34.7 4.3 multiply_reduce_fusion.6
  41.3 5.0 copy.28
  46.3 8.5 %fusion.52 = f32[32768,64]{0,1:T(8,128)S(1)} fusion(f32[64,32768]{1,0:T(8,128)S(1)} %bitcast.142), kind=kOutput, calls=%fused_computation.23.clone.1 | convolution fusion | flops 1610620928 | bytes 16777216 | tf_op jit(solution)/shard_map/while/body/eval_jaxpr/dot_general | solution.py:52
  54.8 5.0 copy.29
  59.9 4.3 multiply_reduce_fusion.6
  66.4 5.0 copy.28
  71.5 8.5 %fusion.52 = f32[32768,64]{0,1:T(8,128)S(1)} fusion(f32[64,32768]{1,0:T(8,128)S(1)} %bitcast.142), kind=kOutput, calls=%fused_computation.23.clone.1 | convolution fusion | flops 1610620928 | bytes 16777216 | tf_op jit(solution)/shard_map/while/body/eval_jaxpr/dot_general | solution.py:52
  80.0 5.0 copy.29
  85.0 4.3 multiply_reduce_fusion.6
  91.6 5.0 copy.28
  96.6 8.5 %fusion.52 = f32[32768,64]{0,1:T(8,128)S(1)} fusion(f32[64,32768]{1,0:T(8,128)S(1)} %bitcast.142), kind=kOutput, calls=%fused_computation.23.clone.1 | convolution fusion | flops 1610620928 | bytes 16777216 | tf_op jit(solution)/shard_map/while/body/eval_jaxpr/dot_general | solution.py:52
  105.1 5.0 copy.29
  110.2 4.3 multiply_reduce_fusion.6
  117.6 136.5 %all-gather.13.cloned.1.call-done = bf16[8192,2048]{1,0:T(8,128)(2,1)} async-done(((bf16[1024,2048]{1,0:T(8,128)(2,1)}), bf16[8192,2048]{1,0:T(8,128)(2,1)}) %all-gather.13.cloned.1.call-update) | async-done | bytes 33554448 | tf_op jit(solution)/shard_map/all_gather | solution.py:65
  254.1 17.9 %convert_multiply_fusion.4 = (f32[256,2048]{1,0:T(8,128)}, f32[256,2048]{1,0:T(8,128)}) fusion(bf16[256,2048]{1,0:T(8,128)(2,1)} %param.16, bf16[256,8192]{1,0:T(8,128)(2,1)} %all-gather.11.cloned.1.call-done, bf16[8192,2048]{1,0:T(8,128)(2,1)} %all-gather.13.cloned.1.call-done), kind=kOutput, calls=%fused_computation.57 | convolution fusion | flops 8590983168 | bytes 42991616 | tf_op jit(solution)/shard_map/dot_general | solution.py:63
  274.3 343.8 %while.68 = (s32[]{:T(128)}, f32[16,2048]{1,0:T(8,128)}, f32[16,2048]{1,0:T(8,128)}, f32[4,64,2048]{2,1,0:T(8,128)}, f32[4,64,2048]{2,1,0:T(8,128)}, /*index=5*/...) while((s32[]{:T(128)}, f32[16,2048]{1,0:T(8,128)}, ...), condition=%wide.region_9.10_spmd.clone.clone.clone, body=%wide.region_6.0_spmd.clone.clone.clone.sunk | while | flops 1639882752 | bytes 212862208 | solution.py:81
  278.7 4.7 copy.30
  283.5 8.8 %fusion.55 = f32[32768,64]{0,1:T(8,128)S(1)} fusion(f32[64,32768]{1,0:T(8,128)S(1)} %bitcast.144), kind=kOutput, calls=%fused_computation.41.clone.1 | convolution fusion | flops 1610620928 | bytes 16777216 | tf_op jit(solution)/shard_map/while/body/eval_jaxpr/dot_general | solution.py:74
  292.3 8.0 %copy.31 = f32[8,8,16,2048]{3,2,1,0:T(8,128)} copy(f32[8,8,16,2048]{3,1,2,0:T(8,128)S(1)} %bitcast.141) | data formatting | bytes 16777216 | tf_op jit(solution)/shard_map/while
  300.3 10.9 %multiply_reduce_fusion.7 = (f32[64,2048]{1,0:T(8,128)S(1)}, f32[64,16,2048]{2,1,0:T(8,128)}, f32[64,16,2048]{2,1,0:T(8,128)S(1)}, f32[64,16,2048]{2,1,0:T(8,128)}) fusion(f32[16,2048]{1,0:T(8,128)} %copy-done.7, f32[16,2048]{1,0:T(8,128)} %get-tuple-element.1005, f32[64]{0:T(128)S(1)} %get-tuple-element.1028, f32[16,2048]{1,0:T(8,128)} %copy-done, ...), kind=kLoop, calls=%fused_computation.35.clone.1 | loop fusion | flops 14548992 | bytes 34603520 | tf_op jit(solution)/shard_map/while/body/eval_jaxpr/reduce_sum | solution.py:79
  312.8 4.3 mul.700
  317.1 11.7 %copy.32 = f32[8,8,16,2048]{3,1,2,0:T(8,128)} copy(f32[8,8,16,2048]{3,2,1,0:T(8,128)} %bitcast.149) | data formatting | bytes 16777216 | tf_op jit(solution)/shard_map/while
  328.7 11.7 %copy.33 = f32[8,8,16,2048]{3,1,2,0:T(8,128)} copy(f32[8,8,16,2048]{3,2,1,0:T(8,128)} %bitcast.146) | data formatting | bytes 16777216 | tf_op jit(solution)/shard_map/while
  340.4 8.2 %copy.34 = f32[8,8,16,2048]{3,1,2,0:T(8,128)} copy(f32[8,8,16,2048]{3,2,1,0:T(8,128)S(1)} %bitcast.145) | data formatting | bytes 16777216 | tf_op jit(solution)/shard_map/while
  348.6 9.5 %fusion.56 = f32[32768]{0:T(1024)S(1)} fusion(f32[64,32768]{1,0:T(8,128)} %bitcast.150, f32[64,32768]{1,0:T(8,128)} %bitcast.151, f32[32768,64]{0,1:T(8,128)S(1)} %fusion.55, f32[64,32768]{1,0:T(8,128)} %bitcast.152, f32[32768]{0:T(1024)S(1)} %bitcast.154), kind=kLoop, calls=%fused_computation.31.clone.1 | loop fusion | flops 10452992 | bytes 33816576 | tf_op jit(solution)/shard_map/while/body/eval_jaxpr/reduce_sum | solution.py:78
  363.6 4.7 copy.30
  368.4 9.0 %fusion.55 = f32[32768,64]{0,1:T(8,128)S(1)} fusion(f32[64,32768]{1,0:T(8,128)S(1)} %bitcast.144), kind=kOutput, calls=%fused_computation.41.clone.1 | convolution fusion | flops 1610620928 | bytes 16777216 | tf_op jit(solution)/shard_map/while/body/eval_jaxpr/dot_general | solution.py:74
  377.4 8.0 %copy.31 = f32[8,8,16,2048]{3,2,1,0:T(8,128)} copy(f32[8,8,16,2048]{3,1,2,0:T(8,128)S(1)} %bitcast.141) | data formatting | bytes 16777216 | tf_op jit(solution)/shard_map/while
  385.4 10.7 %multiply_reduce_fusion.7 = (f32[64,2048]{1,0:T(8,128)S(1)}, f32[64,16,2048]{2,1,0:T(8,128)}, f32[64,16,2048]{2,1,0:T(8,128)S(1)}, f32[64,16,2048]{2,1,0:T(8,128)}) fusion(f32[16,2048]{1,0:T(8,128)} %copy-done.7, f32[16,2048]{1,0:T(8,128)} %get-tuple-element.1005, f32[64]{0:T(128)S(1)} %get-tuple-element.1028, f32[16,2048]{1,0:T(8,128)} %copy-done, ...), kind=kLoop, calls=%fused_computation.35.clone.1 | loop fusion | flops 14548992 | bytes 34603520 | tf_op jit(solution)/shard_map/while/body/eval_jaxpr/reduce_sum | solution.py:79
  397.6 4.3 mul.700
  402.0 11.7 %copy.32 = f32[8,8,16,2048]{3,1,2,0:T(8,128)} copy(f32[8,8,16,2048]{3,2,1,0:T(8,128)} %bitcast.149) | data formatting | bytes 16777216 | tf_op jit(solution)/shard_map/while
  413.6 11.7 %copy.33 = f32[8,8,16,2048]{3,1,2,0:T(8,128)} copy(f32[8,8,16,2048]{3,2,1,0:T(8,128)} %bitcast.146) | data formatting | bytes 16777216 | tf_op jit(solution)/shard_map/while
  425.3 8.2 %copy.34 = f32[8,8,16,2048]{3,1,2,0:T(8,128)} copy(f32[8,8,16,2048]{3,2,1,0:T(8,128)S(1)} %bitcast.145) | data formatting | bytes 16777216 | tf_op jit(solution)/shard_map/while
  433.6 9.5 %fusion.56 = f32[32768]{0:T(1024)S(1)} fusion(f32[64,32768]{1,0:T(8,128)} %bitcast.150, f32[64,32768]{1,0:T(8,128)} %bitcast.151, f32[32768,64]{0,1:T(8,128)S(1)} %fusion.55, f32[64,32768]{1,0:T(8,128)} %bitcast.152, f32[32768]{0:T(1024)S(1)} %bitcast.154), kind=kLoop, calls=%fused_computation.31.clone.1 | loop fusion | flops 10452992 | bytes 33816576 | tf_op jit(solution)/shard_map/while/body/eval_jaxpr/reduce_sum | solution.py:78
  448.7 4.7 copy.30
  453.5 8.8 %fusion.55 = f32[32768,64]{0,1:T(8,128)S(1)} fusion(f32[64,32768]{1,0:T(8,128)S(1)} %bitcast.144), kind=kOutput, calls=%fused_computation.41.clone.1 | convolution fusion | flops 1610620928 | bytes 16777216 | tf_op jit(solution)/shard_map/while/body/eval_jaxpr/dot_general | solution.py:74
  462.2 8.0 %copy.31 = f32[8,8,16,2048]{3,2,1,0:T(8,128)} copy(f32[8,8,16,2048]{3,1,2,0:T(8,128)S(1)} %bitcast.141) | data formatting | bytes 16777216 | tf_op jit(solution)/shard_map/while
  470.2 10.7 %multiply_reduce_fusion.7 = (f32[64,2048]{1,0:T(8,128)S(1)}, f32[64,16,2048]{2,1,0:T(8,128)}, f32[64,16,2048]{2,1,0:T(8,128)S(1)}, f32[64,16,2048]{2,1,0:T(8,128)}) fusion(f32[16,2048]{1,0:T(8,128)} %copy-done.7, f32[16,2048]{1,0:T(8,128)} %get-tuple-element.1005, f32[64]{0:T(128)S(1)} %get-tuple-element.1028, f32[16,2048]{1,0:T(8,128)} %copy-done, ...), kind=kLoop, calls=%fused_computation.35.clone.1 | loop fusion | flops 14548992 | bytes 34603520 | tf_op jit(solution)/shard_map/while/body/eval_jaxpr/reduce_sum | solution.py:79
  482.5 4.3 mul.700
  486.8 11.7 %copy.32 = f32[8,8,16,2048]{3,1,2,0:T(8,128)} copy(f32[8,8,16,2048]{3,2,1,0:T(8,128)} %bitcast.149) | data formatting | bytes 16777216 | tf_op jit(solution)/shard_map/while
  498.5 11.7 %copy.33 = f32[8,8,16,2048]{3,1,2,0:T(8,128)} copy(f32[8,8,16,2048]{3,2,1,0:T(8,128)} %bitcast.146) | data formatting | bytes 16777216 | tf_op jit(solution)/shard_map/while
  510.2 8.4 %copy.34 = f32[8,8,16,2048]{3,1,2,0:T(8,128)} copy(f32[8,8,16,2048]{3,2,1,0:T(8,128)S(1)} %bitcast.145) | data formatting | bytes 16777216 | tf_op jit(solution)/shard_map/while
  518.6 9.5 %fusion.56 = f32[32768]{0:T(1024)S(1)} fusion(f32[64,32768]{1,0:T(8,128)} %bitcast.150, f32[64,32768]{1,0:T(8,128)} %bitcast.151, f32[32768,64]{0,1:T(8,128)S(1)} %fusion.55, f32[64,32768]{1,0:T(8,128)} %bitcast.152, f32[32768]{0:T(1024)S(1)} %bitcast.154), kind=kLoop, calls=%fused_computation.31.clone.1 | loop fusion | flops 10452992 | bytes 33816576 | tf_op jit(solution)/shard_map/while/body/eval_jaxpr/reduce_sum | solution.py:78
  533.5 4.7 copy.30
  538.3 8.8 %fusion.55 = f32[32768,64]{0,1:T(8,128)S(1)} fusion(f32[64,32768]{1,0:T(8,128)S(1)} %bitcast.144), kind=kOutput, calls=%fused_computation.41.clone.1 | convolution fusion | flops 1610620928 | bytes 16777216 | tf_op jit(solution)/shard_map/while/body/eval_jaxpr/dot_general | solution.py:74
  547.1 8.0 %copy.31 = f32[8,8,16,2048]{3,2,1,0:T(8,128)} copy(f32[8,8,16,2048]{3,1,2,0:T(8,128)S(1)} %bitcast.141) | data formatting | bytes 16777216 | tf_op jit(solution)/shard_map/while
  555.1 10.9 %multiply_reduce_fusion.7 = (f32[64,2048]{1,0:T(8,128)S(1)}, f32[64,16,2048]{2,1,0:T(8,128)}, f32[64,16,2048]{2,1,0:T(8,128)S(1)}, f32[64,16,2048]{2,1,0:T(8,128)}) fusion(f32[16,2048]{1,0:T(8,128)} %copy-done.7, f32[16,2048]{1,0:T(8,128)} %get-tuple-element.1005, f32[64]{0:T(128)S(1)} %get-tuple-element.1028, f32[16,2048]{1,0:T(8,128)} %copy-done, ...), kind=kLoop, calls=%fused_computation.35.clone.1 | loop fusion | flops 14548992 | bytes 34603520 | tf_op jit(solution)/shard_map/while/body/eval_jaxpr/reduce_sum | solution.py:79
  567.5 4.3 mul.700
  571.9 11.7 %copy.32 = f32[8,8,16,2048]{3,1,2,0:T(8,128)} copy(f32[8,8,16,2048]{3,2,1,0:T(8,128)} %bitcast.149) | data formatting | bytes 16777216 | tf_op jit(solution)/shard_map/while
  583.5 11.7 %copy.33 = f32[8,8,16,2048]{3,1,2,0:T(8,128)} copy(f32[8,8,16,2048]{3,2,1,0:T(8,128)} %bitcast.146) | data formatting | bytes 16777216 | tf_op jit(solution)/shard_map/while
  595.2 8.2 %copy.34 = f32[8,8,16,2048]{3,1,2,0:T(8,128)} copy(f32[8,8,16,2048]{3,2,1,0:T(8,128)S(1)} %bitcast.145) | data formatting | bytes 16777216 | tf_op jit(solution)/shard_map/while
  603.4 9.5 %fusion.56 = f32[32768]{0:T(1024)S(1)} fusion(f32[64,32768]{1,0:T(8,128)} %bitcast.150, f32[64,32768]{1,0:T(8,128)} %bitcast.151, f32[32768,64]{0,1:T(8,128)S(1)} %fusion.55, f32[64,32768]{1,0:T(8,128)} %bitcast.152, f32[32768]{0:T(1024)S(1)} %bitcast.154), kind=kLoop, calls=%fused_computation.31.clone.1 | loop fusion | flops 10452992 | bytes 33816576 | tf_op jit(solution)/shard_map/while/body/eval_jaxpr/reduce_sum | solution.py:78
  618.3 13.6 %while.65 = (s32[]{:T(128)}, f32[16,2048]{1,0:T(8,128)}, s32[]{:T(128)}, f32[8,16,2048]{2,1,0:T(8,128)}, f32[8,16,2048]{2,1,0:T(8,128)}, /*index=5*/s32[]{:T(128)}, s32[]{:T(128)}) while((s32[]{:T(128)}, f32[16,2048]{1,0:T(8,128)}, s32[]{:T(128)}, f32[8,16,2048]{2,1,0:T(8,128)}, f32[8,16,2048]{2,1,0:T(8,128)}, ...), condition=%wide.region_4.5_spmd.clone, body=%wide.region_3.4_spmd.clone.sunk | while | flops 131076 | bytes 524397 | solution.py:22
  631.8 9.8 %all-gather.19.cloned.1.call-done = f32[128,2048]{1,0:T(8,128)} async-done(((f32[16,2048]{1,0:T(8,128)}), f32[128,2048]{1,0:T(8,128)}) %all-gather.19.cloned.1.call-update) | async-done | bytes 1048592 | tf_op jit(solution)/shard_map/all_gather | solution.py:9
  641.7 13.5 %while.66 = (s32[]{:T(128)}, f32[16,2048]{1,0:T(8,128)}, s32[]{:T(128)}, f32[8,16,2048]{2,1,0:T(8,128)}, f32[8,16,2048]{2,1,0:T(8,128)}, /*index=5*/s32[]{:T(128)}, s32[]{:T(128)}, s32[]{:T(128)}, s32[]{:T(128)}) while((s32[]{:T(128)}, f32[16,2048]{1,0:T(8,128)}, s32[]{:T(128)}, f32[8,16,2048]{2,1,0:T(8,128)}, ...), condition=%wide.region_11.12_spmd.clone, body=%wide.region_10.11_spmd.clone.sunk | while | flops 131080 | bytes 524459 | solution.py:22
  655.2 1.9 add_multiply_fusion
  657.1 21.9 %multiply_reduce_fusion.2 = (f32[256,2048]{1,0:T(8,128)S(1)}, f32[256,2048]{1,0:T(8,128)S(1)}) fusion(f32[16,2048]{1,0:T(8,128)S(1)} %get-tuple-element.781, f32[256]{0:T(256)S(1)} %copy-done.20, f32[16,2048]{1,0:T(8,128)S(1)} %get-tuple-element.1117, f32[16,2048]{1,0:T(8,128)S(1)} %get-tuple-element.782, f32[256]{0:T(256)} %convert_add_fusion), kind=kLoop, calls=%fused_computation.44 | loop fusion | flops 49283072 | bytes 4589568 | tf_op jit(solution)/shard_map/reduce_sum | solution.py:99
  679.2 3.0 fusion.27
  682.1 1.9 reduce_sum.64
  (197 shorter events, 72.8 us)
Async XLA Ops:
  7.2 7.6 %copy-start.4 = (f32[16,2048]{1,0:T(8,128)S(1)}, f32[16,2048]{1,0:T(8,128)}, u32[]{:S(2)}) copy-start(f32[16,2048]{1,0:T(8,128)} %param.22) | copy-start | bytes 393220
  7.2 110.4 %all-gather.11.cloned.1.call-start = ((), (), s32[]{:S(2)}) async-start(), calls=%async_computation | async-start | bytes 5242880 | tf_op jit(solution)/shard_map/all_gather | solution.py:62
  7.9 246.2 %all-gather.13.cloned.1.call-start = ((), (), s32[]{:S(2)}) async-start(), calls=%async_computation.1 | async-start | bytes 37748736 | tf_op jit(solution)/shard_map/all_gather | solution.py:65
  8.7 609.6 %all-gather.15.cloned.1.call-start = ((), (), s32[]{:S(2)}) async-start(), calls=%async_computation.2 | async-start | bytes 1179648 | tf_op jit(solution)/shard_map/all_gather | solution.py:9
  10.5 607.8 %all-gather.17.cloned.1.call-start = ((), (), s32[]{:S(2)}) async-start(), calls=%async_computation.3 | async-start | bytes 1179648 | tf_op jit(solution)/shard_map/all_gather | solution.py:9
  11.2 1.9 copy-start.18
  115.7 0.7 copy-start.10
  116.3 525.3 %all-gather.19.cloned.1.call-start = ((), (), s32[]{:S(2)}) async-start(), calls=%async_computation.4 | async-start | bytes 1179648 | tf_op jit(solution)/shard_map/all_gather | solution.py:9
  274.3 382.8 %copy-start.20 = (f32[256]{0:T(256)S(1)}, f32[256]{0:T(256)}, u32[]{:S(2)}) copy-start(f32[256]{0:T(256)} %convert_subtract_fusion) | copy-start | bytes 3076
  274.5 4.2 copy-start
  274.5 4.2 copy-start.2
  274.5 4.2 copy-start.5
  274.5 4.2 copy-start.7
  340.4 8.2 %copy-start.9 = (f32[2,16,8,128]{3,1,2,0:T(8,128)S(1)}, f32[2,16,8,128]{3,1,2,0:T(8,128)}, u32[]{:S(2)}) copy-start(f32[2,16,8,128]{3,1,2,0:T(8,128)} %copy.35) | copy-start | bytes 393220 | tf_op jit(solution)/shard_map/while
  348.6 9.5 %copy-start.13 = (f32[16,2048]{1,0:T(8,128)S(1)}, f32[16,2048]{1,0:T(8,128)}, u32[]{:S(2)}) copy-start(f32[16,2048]{1,0:T(8,128)} %get-tuple-element.1006) | copy-start | bytes 393220 | tf_op jit(solution)/shard_map/while
  348.6 10.5 %copy-start.1 = (f32[16,2048]{1,0:T(8,128)S(1)}, f32[16,2048]{1,0:T(8,128)}, u32[]{:S(2)}) copy-start(f32[16,2048]{1,0:T(8,128)} %copy-done) | copy-start | bytes 393220 | tf_op jit(solution)/shard_map/while
  348.6 10.5 %copy-start.3 = (f32[4,64,2048]{2,1,0:T(8,128)S(1)}, f32[4,64,2048]{2,1,0:T(8,128)}, u32[]{:S(2)}) copy-start(f32[4,64,2048]{2,1,0:T(8,128)} %copy-done.2) | copy-start | bytes 6291460 | tf_op jit(solution)/shard_map/while
  348.6 10.5 %copy-start.6 = (f32[16,2048]{1,0:T(8,128)S(1)}, f32[16,2048]{1,0:T(8,128)}, u32[]{:S(2)}) copy-start(f32[16,2048]{1,0:T(8,128)} %copy-done.5) | copy-start | bytes 393220 | tf_op jit(solution)/shard_map/while
  348.6 10.5 %copy-start.8 = (f32[16,2048]{1,0:T(8,128)S(1)}, f32[16,2048]{1,0:T(8,128)}, u32[]{:S(2)}) copy-start(f32[16,2048]{1,0:T(8,128)} %copy-done.7) | copy-start | bytes 393220 | tf_op jit(solution)/shard_map/while
  358.2 0.9 copy-start.14
  359.4 4.2 copy-start
  359.4 4.2 copy-start.2
  359.4 4.2 copy-start.5
  359.4 4.2 copy-start.7
  425.3 8.2 %copy-start.9 = (f32[2,16,8,128]{3,1,2,0:T(8,128)S(1)}, f32[2,16,8,128]{3,1,2,0:T(8,128)}, u32[]{:S(2)}) copy-start(f32[2,16,8,128]{3,1,2,0:T(8,128)} %copy.35) | copy-start | bytes 393220 | tf_op jit(solution)/shard_map/while
  433.5 9.5 %copy-start.13 = (f32[16,2048]{1,0:T(8,128)S(1)}, f32[16,2048]{1,0:T(8,128)}, u32[]{:S(2)}) copy-start(f32[16,2048]{1,0:T(8,128)} %get-tuple-element.1006) | copy-start | bytes 393220 | tf_op jit(solution)/shard_map/while
  433.5 10.5 %copy-start.1 = (f32[16,2048]{1,0:T(8,128)S(1)}, f32[16,2048]{1,0:T(8,128)}, u32[]{:S(2)}) copy-start(f32[16,2048]{1,0:T(8,128)} %copy-done) | copy-start | bytes 393220 | tf_op jit(solution)/shard_map/while
  433.5 10.5 %copy-start.3 = (f32[4,64,2048]{2,1,0:T(8,128)S(1)}, f32[4,64,2048]{2,1,0:T(8,128)}, u32[]{:S(2)}) copy-start(f32[4,64,2048]{2,1,0:T(8,128)} %copy-done.2) | copy-start | bytes 6291460 | tf_op jit(solution)/shard_map/while
  433.5 10.5 %copy-start.6 = (f32[16,2048]{1,0:T(8,128)S(1)}, f32[16,2048]{1,0:T(8,128)}, u32[]{:S(2)}) copy-start(f32[16,2048]{1,0:T(8,128)} %copy-done.5) | copy-start | bytes 393220 | tf_op jit(solution)/shard_map/while
  433.5 10.5 %copy-start.8 = (f32[16,2048]{1,0:T(8,128)S(1)}, f32[16,2048]{1,0:T(8,128)}, u32[]{:S(2)}) copy-start(f32[16,2048]{1,0:T(8,128)} %copy-done.7) | copy-start | bytes 393220 | tf_op jit(solution)/shard_map/while
  443.1 0.9 copy-start.14
  444.4 4.2 copy-start
  444.4 4.2 copy-start.2
  444.4 4.2 copy-start.5
  444.5 4.2 copy-start.7
  510.2 8.4 %copy-start.9 = (f32[2,16,8,128]{3,1,2,0:T(8,128)S(1)}, f32[2,16,8,128]{3,1,2,0:T(8,128)}, u32[]{:S(2)}) copy-start(f32[2,16,8,128]{3,1,2,0:T(8,128)} %copy.35) | copy-start | bytes 393220 | tf_op jit(solution)/shard_map/while
  518.6 9.5 %copy-start.13 = (f32[16,2048]{1,0:T(8,128)S(1)}, f32[16,2048]{1,0:T(8,128)}, u32[]{:S(2)}) copy-start(f32[16,2048]{1,0:T(8,128)} %get-tuple-element.1006) | copy-start | bytes 393220 | tf_op jit(solution)/shard_map/while
  518.6 10.4 %copy-start.1 = (f32[16,2048]{1,0:T(8,128)S(1)}, f32[16,2048]{1,0:T(8,128)}, u32[]{:S(2)}) copy-start(f32[16,2048]{1,0:T(8,128)} %copy-done) | copy-start | bytes 393220 | tf_op jit(solution)/shard_map/while
  518.6 10.4 %copy-start.3 = (f32[4,64,2048]{2,1,0:T(8,128)S(1)}, f32[4,64,2048]{2,1,0:T(8,128)}, u32[]{:S(2)}) copy-start(f32[4,64,2048]{2,1,0:T(8,128)} %copy-done.2) | copy-start | bytes 6291460 | tf_op jit(solution)/shard_map/while
  518.6 10.4 %copy-start.6 = (f32[16,2048]{1,0:T(8,128)S(1)}, f32[16,2048]{1,0:T(8,128)}, u32[]{:S(2)}) copy-start(f32[16,2048]{1,0:T(8,128)} %copy-done.5) | copy-start | bytes 393220 | tf_op jit(solution)/shard_map/while
  518.6 10.4 %copy-start.8 = (f32[16,2048]{1,0:T(8,128)S(1)}, f32[16,2048]{1,0:T(8,128)}, u32[]{:S(2)}) copy-start(f32[16,2048]{1,0:T(8,128)} %copy-done.7) | copy-start | bytes 393220 | tf_op jit(solution)/shard_map/while
  528.2 0.8 copy-start.14
  529.2 4.2 copy-start
  529.2 4.2 copy-start.2
  529.3 4.2 copy-start.5
  529.3 4.2 copy-start.7
  595.2 8.2 %copy-start.9 = (f32[2,16,8,128]{3,1,2,0:T(8,128)S(1)}, f32[2,16,8,128]{3,1,2,0:T(8,128)}, u32[]{:S(2)}) copy-start(f32[2,16,8,128]{3,1,2,0:T(8,128)} %copy.35) | copy-start | bytes 393220 | tf_op jit(solution)/shard_map/while
  603.4 9.5 %copy-start.13 = (f32[16,2048]{1,0:T(8,128)S(1)}, f32[16,2048]{1,0:T(8,128)}, u32[]{:S(2)}) copy-start(f32[16,2048]{1,0:T(8,128)} %get-tuple-element.1006) | copy-start | bytes 393220 | tf_op jit(solution)/shard_map/while
  603.4 10.5 %copy-start.1 = (f32[16,2048]{1,0:T(8,128)S(1)}, f32[16,2048]{1,0:T(8,128)}, u32[]{:S(2)}) copy-start(f32[16,2048]{1,0:T(8,128)} %copy-done) | copy-start | bytes 393220 | tf_op jit(solution)/shard_map/while
  603.4 10.5 %copy-start.3 = (f32[4,64,2048]{2,1,0:T(8,128)S(1)}, f32[4,64,2048]{2,1,0:T(8,128)}, u32[]{:S(2)}) copy-start(f32[4,64,2048]{2,1,0:T(8,128)} %copy-done.2) | copy-start | bytes 6291460 | tf_op jit(solution)/shard_map/while
  603.4 10.5 %copy-start.6 = (f32[16,2048]{1,0:T(8,128)S(1)}, f32[16,2048]{1,0:T(8,128)}, u32[]{:S(2)}) copy-start(f32[16,2048]{1,0:T(8,128)} %copy-done.5) | copy-start | bytes 393220 | tf_op jit(solution)/shard_map/while
  603.4 10.5 %copy-start.8 = (f32[16,2048]{1,0:T(8,128)S(1)}, f32[16,2048]{1,0:T(8,128)}, u32[]{:S(2)}) copy-start(f32[16,2048]{1,0:T(8,128)} %copy-done.7) | copy-start | bytes 393220 | tf_op jit(solution)/shard_map/while
  613.0 0.9 copy-start.14
  618.2 64.0 %all-gather.21.cloned.1.call-start = ((), (), s32[]{:S(2)}) async-start(), calls=%async_computation.5 | async-start | bytes 1179648 | tf_op jit(solution)/shard_map/all_gather | solution.py:108
  657.1 22.0 %copy-start.11 = (f32[4,64,2048]{2,1,0:T(8,128)S(1)}, f32[4,64,2048]{2,1,0:T(8,128)}, u32[]{:S(2)}) copy-start(f32[4,64,2048]{2,1,0:T(8,128)} %get-tuple-element.500) | copy-start | bytes 6291460
  657.1 22.0 %copy-start.12 = (f32[4,64,2048]{2,1,0:T(8,128)S(1)}, f32[4,64,2048]{2,1,0:T(8,128)}, u32[]{:S(2)}) copy-start(f32[4,64,2048]{2,1,0:T(8,128)} %get-tuple-element.497) | copy-start | bytes 6291460
  657.1 22.0 %copy-start.15 = (bf16[256,2048]{1,0:T(8,128)(2,1)S(1)}, bf16[256,2048]{1,0:T(8,128)(2,1)}, u32[]{:S(2)}) copy-start(bf16[256,2048]{1,0:T(8,128)(2,1)} %param.17) | copy-start | bytes 3145732
  657.1 22.0 %copy-start.16 = (bf16[256,2048]{1,0:T(8,128)(2,1)S(1)}, bf16[256,2048]{1,0:T(8,128)(2,1)}, u32[]{:S(2)}) copy-start(bf16[256,2048]{1,0:T(8,128)(2,1)} %param.18) | copy-start | bytes 3145732
  657.1 22.0 %copy-start.17 = (f32[256,2048]{1,0:T(8,128)S(1)}, f32[256,2048]{1,0:T(8,128)}, u32[]{:S(2)}) copy-start(f32[256,2048]{1,0:T(8,128)} %get-tuple-element.788) | copy-start | bytes 6291460
  657.1 22.0 %copy-start.19 = (f32[256]{0:T(256)S(1)}, f32[256]{0:T(256)}, u32[]{:S(2)}) copy-start(f32[256]{0:T(256)} %copy-done.18) | copy-start | bytes 3076
Sparse Core Ops, SparseCore 0:
  9.6 83.4 all-gather.10
  94.9 159.1 all-gather.12
  256.6 23.3 all-gather.14
  282.3 23.3 all-gather.16
  618.3 23.3 all-gather.18
  657.2 23.3 all-gather.20
